TPU v7x, 32 devices: a whole 2x2x4 slice. The times are simulated.
32 devices in a mesh: wide: 16 (over z, x, core), narrow: 2 (over y).
Axes of the slice: x: 2, y: 2, z: 4, core: 2. Of those that a mesh axis runs over, the one named last changes fastest.
Arguments:
- activations: float32 [1024, 17408], P('wide', 'narrow'), may hold values from -6 to 6
- act_basis: float32 [17408, 17408], P('narrow', 'wide'), may hold values from -0.046875 to 0.046875
- grads: float32 [1024, 5120], P(None, 'wide'), may hold values from -0.3 to 0.3
- grad_basis: float32 [5120, 5120], P('wide', 'narrow'), may hold values from -0.078125 to 0.078125
- seq_ids: int32 [1024], replicated, may hold values from 0 to 3, never falling along the last dimension, each value on 1 to 512 neighbouring positions
Outputs:
- eigenvalues: float32 [17408, 5120], P('wide', 'narrow')
Inputs may be any that keep to these rules, and one draw needn't show every extreme that they name: `seq_ids`: never falling along the rows; every sequence has at least one row and at most 512 rows, and one sequence has exactly 512.
All inputs are finite; a program needn't handle non-finite values.
Results may differ from a plain program's by a relative error of at most 0.0003.
Values sent between devices are 32-bit elements; how exact they have to be, the bound alone decides.
A program may use at most 192 MiB of HBM per device.

v0:
```python
import jax
import jax.numpy as jnp
from jax import lax
from jax.sharding import PartitionSpec as P

SEQS = 4
SEQ_MOST = 512


def seq_window(rotated_acts, rotated_grads, seq_ids, seq_label):
    token_rows = rotated_grads.shape[0]
    first_row = jnp.sum((seq_ids < seq_label).astype(jnp.int32))
    window_start = jnp.minimum(first_row, token_rows - SEQ_MOST)
    acts_window = lax.dynamic_slice_in_dim(rotated_acts, window_start, SEQ_MOST, 0)
    grads_window = lax.dynamic_slice_in_dim(rotated_grads, window_start, SEQ_MOST, 0)
    ids_window = lax.dynamic_slice_in_dim(seq_ids, window_start, SEQ_MOST, 0)
    seq_mask = (ids_window == seq_label).astype(jnp.float32)[:, None]
    return (acts_window, grads_window * seq_mask)


def per_device(activations, act_basis, grads, grad_basis, seq_ids):
    highest = lax.Precision.HIGHEST
    partial_acts = jnp.dot(
        lax.all_gather(activations, "wide", axis=0, tiled=True),
        act_basis,
        precision=highest,
        preferred_element_type=jnp.float32,
    )
    rotated_acts = lax.psum(partial_acts, "narrow")
    partial_grads = jnp.dot(
        grads, grad_basis, precision=highest, preferred_element_type=jnp.float32
    )
    rotated_grads = lax.psum(partial_grads, "wide")
    out_cols = rotated_grads.shape[1]
    running = jnp.zeros((rotated_acts.shape[1], out_cols), jnp.float32)
    for seq_label in range(SEQS):
        acts_window, grads_window = seq_window(rotated_acts, rotated_grads, seq_ids, seq_label)
        moment = jnp.dot(
            acts_window.T, grads_window, precision=highest, preferred_element_type=jnp.float32
        )
        running = running + moment * moment
    return running / jnp.float32(SEQS)


def solution(mesh):
    in_specs = (P("wide", "narrow"), P("narrow", "wide"), P(None, "wide"), P("wide", "narrow"), P())
    out_specs = P("wide", "narrow")
    return jax.shard_map(
        per_device, mesh=mesh, in_specs=in_specs, out_specs=out_specs, check_vma=False
    )
```

profile of v0, /device:TPU:0, one launch (start us, length us, event | category | flops | bytes accessed | tf_op | source)
XLA Modules:
  0.0 607.3 jit_solution(9304746979321440647)
XLA Ops:
  6.5 0.0 copy-start
  6.5 0.0 all-gather.2.cloned.1.call-start
  6.5 0.7 all-gather.2.cloned.1.call-update
  7.3 0.0 all-reduce.5.cloned.1.call-start
  7.3 1.2 copy-done
  8.5 20.3 %fusion.29 = f32[1024,2560]{1,0:T(8,128)} fusion(f32[1024,320]{0,1:T(8,128)} %param.7, f32[320,2560]{1,0:T(8,128)S(1)} %copy-done), kind=kOutput, calls=%fused_computation.41 | convolution fusion | flops 10066329600 | bytes 15073280 | tf_op jit(solution)/shard_map/dot_general | solution.py:30
  28.8 0.0 all-reduce.5.cloned.1.call-update
  28.8 0.0 copy-start.3
  28.8 0.6 all-reduce.3.cloned.1.call-start
  29.4 160.2 %all-gather.2.cloned.1.call-done = f32[1024,8704]{1,0:T(8,128)} async-done(((f32[64,8704]{1,0:T(8,128)}), f32[1024,8704]{1,0:T(8,128)}) %all-gather.2.cloned.1.call-update) | async-done | bytes 35651600 | tf_op jit(solution)/shard_map/all_gather | solution.py:24
  189.6 127.6 %fusion.28 = f32[1024,1088]{0,1:T(8,128)} fusion(f32[1024,8704]{1,0:T(8,128)} %all-gather.2.cloned.1.call-done, f32[8704,1088]{0,1:T(8,128)} %param.6), kind=kOutput, calls=%fused_computation.40 | convolution fusion | flops 116366770176 | bytes 77987840 | tf_op jit(solution)/shard_map/dot_general | solution.py:23
  317.2 0.0 all-reduce.3.cloned.1.call-update
  317.3 0.0 copy-done.3
  317.3 0.7 convert_reduce_fusion
  320.5 0.1 fusion.27
  320.6 73.7 %all-reduce.5.cloned.1.call-done = f32[1024,2560]{1,0:T(8,128)} async-done(((f32[1024,2560]{1,0:T(8,128)}), f32[1024,2560]{1,0:T(8,128)}) %all-reduce.5.cloned.1.call-update) | async-done | bytes 10485776 | tf_op jit(solution)/shard_map/psum | solution.py:33
  394.3 116.0 %all-reduce.3.cloned.1.call-done = f32[1024,1088]{0,1:T(8,128)} async-done(((f32[1024,1088]{0,1:T(8,128)}), f32[1024,1088]{0,1:T(8,128)}) %all-reduce.3.cloned.1.call-update) | async-done | bytes 4456464 | tf_op jit(solution)/shard_map/psum | solution.py:29
  510.4 0.0 copy-start.2
  510.4 22.5 %convolution_multiply_fusion.2 = f32[1088,2560]{1,0:T(8,128)S(1)} fusion(f32[1024,2560]{1,0:T(8,128)} %all-reduce.5.cloned.1.call-done, s32[]{:T(128)S(6)} %select_n.9, f32[512]{0:T(512)S(1)} %get-tuple-element.12, f32[1024,1088]{0,1:T(8,128)} %all-reduce.3.cloned.1.call-done), kind=kOutput, calls=%fused_computation.2 | convolution fusion | flops 17116856320 | bytes 18615296 | tf_op jit(solution)/shard_map/dot_general | solution.py:38
  532.9 0.0 copy-done.2
  532.9 21.9 %fusion = f32[1088,2560]{1,0:T(8,128)S(1)} fusion(f32[1088,2560]{1,0:T(8,128)S(1)} %convolution_multiply_fusion.2, f32[1024,2560]{1,0:T(8,128)} %all-reduce.5.cloned.1.call-done, s32[]{:T(128)S(6)} %select_n.8, f32[512]{0:T(512)S(1)} %get-tuple-element.11, f32[1024,1088]{0,1:T(8,128)S(1)} %copy-done.2), kind=kOutput, calls=%fused_computation.4 | convolution fusion | flops 17119641600 | bytes 29756416 | tf_op jit(solution)/shard_map/dot_general | solution.py:38
  554.8 22.0 %fusion.1 = f32[1088,2560]{1,0:T(8,128)S(1)} fusion(f32[1088,2560]{1,0:T(8,128)S(1)} %fusion, f32[1024,2560]{1,0:T(8,128)} %all-reduce.5.cloned.1.call-done, s32[]{:T(128)S(6)} %select_n.10, f32[512]{0:T(512)S(1)} %get-tuple-element.10, f32[1024,1088]{0,1:T(8,128)S(1)} %copy-done.2), kind=kOutput, calls=%fused_computation.5 | convolution fusion | flops 17119641600 | bytes 29756416 | tf_op jit(solution)/shard_map/dot_general | solution.py:38
  576.8 0.0 copy-start.1
  576.8 23.4 %fusion.3 = f32[1088,2560]{1,0:T(8,128)} fusion(f32[1088,2560]{1,0:T(8,128)S(1)} %fusion.1, f32[1024,2560]{1,0:T(8,128)} %all-reduce.5.cloned.1.call-done, s32[]{:T(128)S(6)} %select_n.11, f32[512]{0:T(512)S(1)} %get-tuple-element.9, f32[1024,1088]{0,1:T(8,128)S(1)} %copy-done.2), kind=kOutput, calls=%fused_computation.7 | convolution fusion | flops 17122426880 | bytes 29756416 | tf_op jit(solution)/shard_map/dot_general | solution.py:38
  600.3 0.0 copy-done.1
Async XLA Ops:
  6.5 1.9 copy-start
  6.5 183.1 %all-gather.2.cloned.1.call-start = ((), (), s32[]{:S(2)}) async-start(), calls=%async_computation | async-start | bytes 37879808 | tf_op jit(solution)/shard_map/all_gather | solution.py:24
  7.3 387.1 %all-reduce.5.cloned.1.call-start = ((), (), s32[]{:S(2)}) async-start(), calls=%async_computation.2 | async-start | bytes 20971520 | tf_op jit(solution)/shard_map/psum | solution.py:33
  28.8 288.4 %copy-start.3 = (s32[1024]{0:T(1024)S(1)}, s32[1024]{0:T(1024)}, u32[]{:S(2)}) copy-start(s32[1024]{0:T(1024)} %param.9) | copy-start | bytes 12292
  28.8 481.5 %all-reduce.3.cloned.1.call-start = ((), (), s32[]{:S(2)}) async-start(), calls=%async_computation.1 | async-start | bytes 8912896 | tf_op jit(solution)/shard_map/psum | solution.py:29
  510.4 22.5 %copy-start.2 = (f32[1024,1088]{0,1:T(8,128)S(1)}, f32[1024,1088]{0,1:T(8,128)}, u32[]{:S(2)}) copy-start(f32[1024,1088]{0,1:T(8,128)} %all-reduce.3.cloned.1.call-done) | copy-start | bytes 13369348
  576.8 23.4 %copy-start.1 = (f32[320,2560]{1,0:T(8,128)S(1)}, f32[320,2560]{1,0:T(8,128)}, u32[]{:S(2)}) copy-start(f32[320,2560]{1,0:T(8,128)} %param.8) | copy-start | bytes 9830404
Sparse Core Ops, SparseCore 0:
  8.9 180.6 all-gather.1
  193.4 200.9 all-reduce.4
  396.8 113.5 all-reduce.2
where the time goes:
time: 614 us; the launch traced here: 607 us
  waiting for transfers between devices  351 us (57%)
  matrix products  238 us (39%)
  between operations  16.2 us (3%)
    all_gather x1, waiting for transfers between devices, per_device(): lax.all_gather(activations, 'wide', axis=0, tiled=True)  160 us
    dot_general x1, matrix products, per_device(): jnp.dot(lax.all_gather(activations, 'wide', axis=0, tiled=True), act_basi...  128 us
    psum x1, waiting for transfers between devices, per_device(): rotated_acts = lax.psum(partial_acts, 'narrow')  116 us
    dot_general x4, matrix products, per_device(): jnp.dot(acts_window.T, grads_window, precision=highest, preferred_element...  89.8 us
    psum x1, waiting for transfers between devices, per_device(): rotated_grads = lax.psum(partial_grads, 'wide')  73.7 us
    dot_general x1, matrix products, per_device(): jnp.dot(grads, grad_basis, precision=highest, preferred_element_type=jnp....  20.3 us
  transfers between devices with their start and end apart: 3, of which 3 were waited for; matrix products, arithmetic and copies ran while one was open for 24% of the time, Pallas kernels for 0%

commit v1 on v0

v1 whole, which is shorter than its diff:
```python
import functools

import jax
import jax.numpy as jnp
from jax import lax
from jax.experimental import pallas as pl
from jax.experimental.pallas import tpu as pltpu
from jax.sharding import PartitionSpec as P

SEQS = 4
SEQ_MOST = 512
MESH = pl.DeviceIdType.MESH


def dot(a, b):
    return jnp.dot(a, b, precision=lax.Precision.HIGH, preferred_element_type=jnp.float32)


def split(value):
    high = value.astype(jnp.bfloat16)
    return high, (value - high.astype(jnp.float32)).astype(jnp.bfloat16)


def three_pass(a, b):
    a_high, a_low = split(a)
    b_high, b_low = split(b)
    contract = (((1,), (1,)), ((), ()))
    mul = functools.partial(lax.dot_general, dimension_numbers=contract, preferred_element_type=jnp.float32)
    return mul(a_high, b_high) + (mul(a_high, b_low) + mul(a_low, b_high))


def depth_tile(depth):
    best = 128
    for tile in range(128, min(depth, 1024) + 1, 128):
        if depth % tile == 0:
            best = tile
    return best


def gather_kernel(line_size, swap, x_ref, u_ref, gathered, part, other, own, acc,
                  send_line, send_pair, send_core, recv, own_sem, out_sem, send_swap, recv_swap):
    rows, depth = x_ref.shape
    group = 4 * rows
    me = lax.axis_index("wide")
    side = lax.axis_index("narrow")
    line, pair, core = me // 4, (me // 2) % 2, me % 2

    def index(l, p, c):
        return (l * 2 + p) * 2 + c

    def wide_id(w):
        return (w, side)

    pair_id = wide_id(index(line, 1 - pair, core))
    core_id = wide_id(index(line, pair, 1 - core))
    left, right = line - 1, line + 1
    has_left, has_right = line > 0, line < line_size - 1

    barrier = pltpu.get_barrier_semaphore()
    pl.semaphore_signal(barrier, inc=1, device_id=pair_id, device_id_type=MESH)
    pl.semaphore_signal(barrier, inc=1, device_id=core_id, device_id_type=MESH)
    if swap:
        pl.semaphore_signal(barrier, inc=1, device_id=(me, 1 - side), device_id_type=MESH)

    @pl.when(has_left)
    def _():
        pl.semaphore_signal(barrier, inc=1, device_id=wide_id(index(left, pair, core)), device_id_type=MESH)

    @pl.when(has_right)
    def _():
        pl.semaphore_signal(barrier, inc=1, device_id=wide_id(index(right, pair, core)), device_id_type=MESH)

    pl.semaphore_wait(
        barrier, (3 if swap else 2) + jnp.minimum(line, 1) + jnp.minimum(line_size - 1 - line, 1)
    )

    def block(w):
        return gathered.at[pl.ds(pl.multiple_of(w * rows, 8), rows), :]

    def send(src, w, sem, target):
        return pltpu.make_async_remote_copy(
            src_ref=src, dst_ref=block(w), send_sem=sem, recv_sem=recv.at[w],
            device_id=target, device_id_type=MESH)

    def line_send(src, l, step):
        return send(src, index(l, pair, core), send_line.at[l],
                    wide_id(index(line + step, pair, core)))

    def pair_send(src, l):
        return send(src, index(l, pair, core), send_pair.at[l], pair_id)

    def core_send(src, l, p):
        return send(src, index(l, p, core), send_core.at[index(l, p, 0) // 2], core_id)

    def wait_block(w):
        pltpu.make_async_copy(block(w), block(w), recv.at[w]).wait()

    own_left = send(x_ref, me, send_line.at[line_size], wide_id(index(left, pair, core)))
    own_right = send(x_ref, me, send_line.at[line], wide_id(index(right, pair, core)))

    @pl.when(has_right)
    def _():
        own_right.start()

    @pl.when(has_left)
    def _():
        own_left.start()

    pair_send(x_ref, line).start()
    core_send(x_ref, line, pair).start()
    load = pltpu.make_async_copy(x_ref, own, own_sem.at[0])
    load.start()
    load.wait()
    store = pltpu.make_async_copy(own, block(me), own_sem.at[1])
    store.start()
    store.wait()

    tile = depth_tile(depth)

    def group_rows(ref, l):
        return ref.at[pl.ds(pl.multiple_of(l * group, 8), group), :]

    def swap_copy(l):
        return pltpu.make_async_remote_copy(
            src_ref=group_rows(part, l), dst_ref=group_rows(other, l),
            send_sem=send_swap.at[l], recv_sem=recv_swap.at[l],
            device_id=(me, 1 - side), device_id_type=MESH)

    def arrive(l, step):
        w = index(l, pair, core)
        wait_block(w)

        @pl.when((line + step >= 0) & (line + step < line_size))
        def _():
            line_send(block(w), l, step).start()

        pair_send(block(w), l).start()
        core_send(block(w), l, pair).start()

    def finish(l):
        crossed = index(l, 1 - pair, core)
        wait_block(crossed)
        core_send(block(crossed), l, 1 - pair).start()
        wait_block(index(l, pair, 1 - core))
        wait_block(index(l, 1 - pair, 1 - core))
        acc[...] = jnp.zeros_like(acc)

        def body(x_tile, u_tile):
            acc[...] += three_pass(x_tile[...], u_tile[...])

        pltpu.emit_pipeline(
            body,
            grid=(depth // tile,),
            in_specs=[
                pl.BlockSpec((group, tile), lambda k: (0, k)),
                pl.BlockSpec((u_ref.shape[0], tile), lambda k: (0, k)),
            ],
        )(group_rows(gathered, l), u_ref)
        out = pltpu.make_async_copy(acc, group_rows(part, l), out_sem)
        out.start()
        out.wait()
        if swap:
            swap_copy(l).start()

    def step(d, carry):
        @pl.when((d < line_size) & (line - d >= 0))
        def _():
            arrive(line - d, 1)

        @pl.when((d < line_size) & (line + d < line_size))
        def _():
            arrive(line + d, -1)

        @pl.when(line - (d - 1) >= 0)
        def _():
            finish(line - (d - 1))

        @pl.when((d > 1) & (line + (d - 1) < line_size))
        def _():
            finish(line + (d - 1))

        return carry

    lax.fori_loop(1, line_size + 1, step, 0)

    def drain(l, carry):
        @pl.when((l <= line) & has_right)
        def _():
            line_send(block(index(l, pair, core)), l, 1).wait_send()

        @pl.when((l > line) & has_left)
        def _():
            line_send(block(index(l, pair, core)), l, -1).wait_send()

        pair_send(block(index(l, pair, core)), l).wait_send()
        core_send(block(index(l, 0, core)), l, 0).wait_send()
        core_send(block(index(l, 1, core)), l, 1).wait_send()
        if swap:
            swap_copy(l).wait()
        return carry

    lax.fori_loop(0, line_size, drain, 0)

    @pl.when(has_left)
    def _():
        own_left.wait_send()


def gather_product(wide, narrow, activations, act_basis):
    rows, depth = activations.shape
    cols = act_basis.shape[1]
    line_size = wide // 4
    swap = narrow == 2
    full = wide * rows
    shape = functools.partial(jax.ShapeDtypeStruct, dtype=jnp.float32)
    hbm = pl.BlockSpec(memory_space=pltpu.HBM)
    gathered, part, other = pl.pallas_call(
        functools.partial(gather_kernel, line_size, swap),
        out_shape=[shape((full, depth)), shape((full, cols)), shape((full, cols))],
        in_specs=[hbm, hbm],
        out_specs=[hbm, hbm, hbm],
        scratch_shapes=[
            pltpu.VMEM((rows, depth), jnp.float32),
            pltpu.VMEM((4 * rows, cols), jnp.float32),
            pltpu.SemaphoreType.DMA((line_size + 1,)),
            pltpu.SemaphoreType.DMA((line_size,)),
            pltpu.SemaphoreType.DMA((2 * line_size,)),
            pltpu.SemaphoreType.DMA((wide,)),
            pltpu.SemaphoreType.DMA((2,)),
            pltpu.SemaphoreType.DMA,
            pltpu.SemaphoreType.DMA((line_size,)),
            pltpu.SemaphoreType.DMA((line_size,)),
        ],
        cost_estimate=pl.CostEstimate(
            flops=6 * full * depth * cols, bytes_accessed=4 * line_size * depth * cols, transcendentals=0),
        compiler_params=pltpu.CompilerParams(
            collective_id=0, has_side_effects=True, vmem_limit_bytes=48 * 1024 * 1024),
    )(activations, act_basis.T)
    return part + other if swap else lax.psum(part, "narrow")


def per_device(wide, narrow, activations, act_basis, grads, grad_basis, seq_ids):
    rotated_grads = lax.psum(dot(grads, grad_basis), "wide")
    rotated_acts = gather_product(wide, narrow, activations, act_basis)
    token_rows = rotated_grads.shape[0]
    running = None
    for seq_label in range(SEQS):
        first_row = jnp.sum((seq_ids < seq_label).astype(jnp.int32))
        start = jnp.minimum(first_row, token_rows - SEQ_MOST)
        ids_window = lax.dynamic_slice_in_dim(seq_ids, start, SEQ_MOST, 0)
        mask = (ids_window == seq_label).astype(jnp.float32)[:, None]
        acts_window = lax.dynamic_slice_in_dim(rotated_acts, start, SEQ_MOST, 0)
        grads_window = lax.dynamic_slice_in_dim(rotated_grads, start, SEQ_MOST, 0) * mask
        moment = dot(acts_window.T, grads_window)
        running = moment * moment if running is None else running + moment * moment
    return running / jnp.float32(SEQS)


def solution(mesh):
    wide, narrow = mesh.shape["wide"], mesh.shape["narrow"]

    def body(*args):
        return per_device(wide, narrow, *args)

    in_specs = (P("wide", "narrow"), P("narrow", "wide"), P(None, "wide"), P("wide", "narrow"), P())
    return jax.shard_map(
        body, mesh=mesh, in_specs=in_specs, out_specs=P("wide", "narrow"), check_vma=False
    )
```

time: 614 us -> 475 us (0.77)
  Pallas kernels: 0 us -> 378 us
  waiting for transfers between devices: 351 us -> 0.02 us
  matrix products: 238 us -> 68.4 us
  other arithmetic: 0.8 us -> 7.19 us
    pallas_call x0 -> x1, Pallas kernels: none -> 378 us  [gather_product(): pl.pallas_call(functools.partial(gather_kernel, line_size, swap), out_sha...]
    psum x2 -> x1, waiting for transfers between devices: 190 us -> 0.01 us  [per_device(): rotated_grads = lax.psum(dot(grads, grad_basis), 'wide')]
    dot_general x6 -> x5, matrix products: 238 us -> 68.4 us  [dot(): jnp.dot(a, b, precision=lax.Precision.HIGH, preferred_element_type=jnp.fl...]
    all_gather x1 -> x0, waiting for transfers between devices: 160 us -> none  [per_device(): lax.all_gather(activations, 'wide', axis=0, tiled=True)]
    add x0 -> x1, other arithmetic: none -> 6.37 us  [gather_product(): return part + other if swap else lax.psum(part, 'narrow')]
  transfers between devices with their start and end apart: 3 -> 1, of which waited for: 3 -> 0; matrix products, arithmetic and copies ran while one was open for 24% -> 2% of each run, Pallas kernels for 0% -> 80%
where the time goes in v1:
time: 475 us; the launch traced here: 472 us
  Pallas kernels  378 us (80%)
  matrix products  68.4 us (14%)
  between operations  16 us (3%)
  other arithmetic  7.19 us (2%)
    pallas_call x1, Pallas kernels, gather_product(): pl.pallas_call(functools.partial(gather_kernel, line_size, swap), out_sha...  378 us
    dot_general x5, matrix products, dot(): jnp.dot(a, b, precision=lax.Precision.HIGH, preferred_element_type=jnp.fl...  68.4 us
  transfers between devices with their start and end apart: 1, of which 0 were waited for; matrix products, arithmetic and copies ran while one was open for 2% of the time, Pallas kernels for 80%

profile of v1, /device:TPU:0, one launch (start us, length us, event | category | flops | bytes accessed | tf_op | source)
XLA Modules:
  0.0 472.0 jit_solution(13406794246959497236)
XLA Ops:
  6.5 0.0 copy-start
  6.5 0.0 all-reduce.2.cloned.1.call-start
  6.5 1.9 copy-done
  8.5 12.3 %fusion.28 = f32[1024,2560]{1,0:T(8,128)} fusion(f32[1024,320]{0,1:T(8,128)} %param.7, f32[320,2560]{1,0:T(8,128)S(1)} %copy-done), kind=kOutput, calls=%fused_computation.40 | convolution fusion | flops 5033164800 | bytes 15073280 | tf_op jit(solution)/shard_map/dot_general | solution.py:16
  20.7 0.0 copy-start.4
  20.7 0.0 copy-start.2
  20.7 0.0 all-reduce.2.cloned.1.call-update
  20.8 0.7 copy-done.4
  21.4 0.7 convert_reduce_fusion
  24.7 0.0 copy-done.2
  24.7 377.8 %shard_map.55 = (f32[1024,8704]{1,0:T(8,128)}, f32[1024,1088]{1,0:T(8,128)}, f32[1024,1088]{1,0:T(8,128)}) custom-call(f32[64,8704]{1,0:T(8,128)S(1)} %copy-done.2, f32[1088,8704]{1,0:T(8,128)} %bitcast.3), custom_call_target="tpu_custom_call" | custom-call | flops 58183385088 | bytes 151519232 | tf_op jit(solution)/shard_map/pallas_call | solution.py:217
  402.5 6.4 %add.34 = f32[1024,1088]{1,0:T(8,128)} add(f32[1024,1088]{1,0:T(8,128)} %get-tuple-element.7, f32[1024,1088]{1,0:T(8,128)} %get-tuple-element.8) | non-fusion elementwise | flops 1114112 | bytes 13369344 | tf_op jit(solution)/shard_map/add | solution.py:239
  408.8 0.1 fusion.27
  408.9 0.0 all-reduce.2.cloned.1.call-done
  408.9 0.0 copy-start.3
  408.9 12.8 %convolution_multiply_fusion.2 = f32[1088,2560]{1,0:T(8,128)S(1)} fusion(f32[1024,2560]{1,0:T(8,128)} %all-reduce.2.cloned.1.call-done, s32[]{:T(128)S(6)} %select_n.9, f32[512]{0:T(512)S(1)} %get-tuple-element.16, f32[1024,1088]{1,0:T(8,128)} %add.34), kind=kOutput, calls=%fused_computation.2 | convolution fusion | flops 8560476160 | bytes 18746368 | tf_op jit(solution)/shard_map/dot_general | solution.py:16
  421.8 0.0 copy-done.3
  421.8 14.5 %fusion = f32[1088,2560]{1,0:T(8,128)} fusion(f32[1088,2560]{1,0:T(8,128)S(1)} %convolution_multiply_fusion.2, f32[1024,2560]{1,0:T(8,128)} %all-reduce.2.cloned.1.call-done, s32[]{:T(128)S(6)} %select_n.8, f32[512]{0:T(512)S(1)} %get-tuple-element.15, f32[1024,1088]{1,0:T(8,128)S(1)} %copy-done.3), kind=kOutput, calls=%fused_computation.4 | convolution fusion | flops 8563261440 | bytes 29887488 | tf_op jit(solution)/shard_map/dot_general | solution.py:16
  436.3 14.0 %fusion.1 = f32[1088,2560]{1,0:T(8,128)S(1)} fusion(f32[1088,2560]{1,0:T(8,128)} %fusion, f32[1024,2560]{1,0:T(8,128)} %all-reduce.2.cloned.1.call-done, s32[]{:T(128)S(6)} %select_n.10, f32[512]{0:T(512)S(1)} %get-tuple-element.14, f32[1024,1088]{1,0:T(8,128)S(1)} %copy-done.3), kind=kOutput, calls=%fused_computation.5 | convolution fusion | flops 8563261440 | bytes 29887488 | tf_op jit(solution)/shard_map/dot_general | solution.py:16
  450.3 0.0 copy-start.1
  450.3 14.9 %fusion.3 = f32[1088,2560]{1,0:T(8,128)} fusion(f32[1088,2560]{1,0:T(8,128)S(1)} %fusion.1, f32[1024,2560]{1,0:T(8,128)} %all-reduce.2.cloned.1.call-done, s32[]{:T(128)S(6)} %select_n.11, f32[512]{0:T(512)S(1)} %get-tuple-element.13, f32[1024,1088]{1,0:T(8,128)S(1)} %copy-done.3), kind=kOutput, calls=%fused_computation.7 | convolution fusion | flops 8566046720 | bytes 29887488 | tf_op jit(solution)/shard_map/dot_general | solution.py:16
  465.1 0.0 copy-done.1
Async XLA Ops:
  6.5 1.9 copy-start
  6.5 402.4 %all-reduce.2.cloned.1.call-start = ((), (), s32[]{:S(2)}) async-start(), calls=%async_computation | async-start | bytes 20971520 | tf_op jit(solution)/shard_map/psum | solution.py:243
  20.7 0.7 copy-start.4
  20.7 4.0 copy-start.2
  408.9 12.9 %copy-start.3 = (f32[1024,1088]{1,0:T(8,128)S(1)}, f32[1024,1088]{1,0:T(8,128)}, u32[]{:S(2)}) copy-start(f32[1024,1088]{1,0:T(8,128)} %add.34) | copy-start | bytes 13369348
  450.3 14.9 %copy-start.1 = (f32[320,2560]{1,0:T(8,128)S(1)}, f32[320,2560]{1,0:T(8,128)}, u32[]{:S(2)}) copy-start(f32[320,2560]{1,0:T(8,128)} %param.8) | copy-start | bytes 9830404
Sparse Core Ops, SparseCore 0:
  20.9 314.1 all-reduce.1

commit v2 on v1

--- a/solution.py
+++ b/solution.py
@@ -243,14 +243,23 @@
     rotated_grads = lax.psum(dot(grads, grad_basis), "wide")
     rotated_acts = gather_product(wide, narrow, activations, act_basis)
     token_rows = rotated_grads.shape[0]
+    counts = [jnp.sum((seq_ids == s).astype(jnp.int32)) for s in range(SEQS)]
+    ranks = [
+        sum(((counts[t] >= counts[s]) if t < s else (counts[t] > counts[s])).astype(jnp.int32)
+            for t in range(SEQS) if t != s)
+        for s in range(SEQS)
+    ]
     running = None
-    for seq_label in range(SEQS):
+    for rank in range(SEQS):
+        most = SEQ_MOST if rank == 0 else (token_rows - SEQ_MOST) // rank
+        window = min(SEQ_MOST, -(-most // 128) * 128)
+        seq_label = sum(s * (ranks[s] == rank).astype(jnp.int32) for s in range(SEQS))
         first_row = jnp.sum((seq_ids < seq_label).astype(jnp.int32))
-        start = jnp.minimum(first_row, token_rows - SEQ_MOST)
-        ids_window = lax.dynamic_slice_in_dim(seq_ids, start, SEQ_MOST, 0)
+        start = jnp.minimum(first_row, token_rows - window)
+        ids_window = lax.dynamic_slice_in_dim(seq_ids, start, window, 0)
         mask = (ids_window == seq_label).astype(jnp.float32)[:, None]
-        acts_window = lax.dynamic_slice_in_dim(rotated_acts, start, SEQ_MOST, 0)
-        grads_window = lax.dynamic_slice_in_dim(rotated_grads, start, SEQ_MOST, 0) * mask
+        acts_window = lax.dynamic_slice_in_dim(rotated_acts, start, window, 0)
+        grads_window = lax.dynamic_slice_in_dim(rotated_grads, start, window, 0) * mask
         moment = dot(acts_window.T, grads_window)
         running = moment * moment if running is None else running + moment * moment
     return running / jnp.float32(SEQS)

time: 475 us -> 482 us (1.015)
  between operations: 16 us -> 27.3 us
  matrix products: 68.4 us -> 60.4 us
    dot_general x5, matrix products: 68.4 us -> 60.4 us  [dot(): jnp.dot(a, b, precision=lax.Precision.HIGH, preferred_element_type=jnp.fl...]
  transfers between devices with their start and end apart: 1 -> 1, of which waited for: 0 -> 0; matrix products, arithmetic and copies ran while one was open for 2% -> 2% of each run, Pallas kernels for 80% -> 79%
where the time goes in v2:
time: 482 us; the launch traced here: 480 us
  Pallas kernels  382 us (79%)
  matrix products  60.4 us (13%)
  between operations  27.3 us (6%)
  other arithmetic  7.99 us (2%)
    pallas_call x1, Pallas kernels, gather_product(): pl.pallas_call(functools.partial(gather_kernel, line_size, swap), out_sha...  382 us
    dot_general x5, matrix products, dot(): jnp.dot(a, b, precision=lax.Precision.HIGH, preferred_element_type=jnp.fl...  60.4 us
  transfers between devices with their start and end apart: 1, of which 0 were waited for; matrix products, arithmetic and copies ran while one was open for 2% of the time, Pallas kernels for 79%

profile of v2, /device:TPU:0, one launch (start us, length us, event | category | flops | bytes accessed | tf_op | source)
XLA Modules:
  0.0 480.0 jit_solution(13850121997123332984)
XLA Ops:
  6.5 0.0 copy-start
  6.5 0.0 all-reduce.2.cloned.1.call-start
  6.5 1.9 copy-done
  8.5 12.3 %fusion.26 = f32[1024,2560]{1,0:T(8,128)} fusion(f32[1024,320]{0,1:T(8,128)} %param.7, f32[320,2560]{1,0:T(8,128)S(1)} %copy-done), kind=kOutput, calls=%fused_computation.42 | convolution fusion | flops 5033164800 | bytes 15073280 | tf_op jit(solution)/shard_map/dot_general | solution.py:16
  20.7 0.0 copy-start.4
  20.7 0.0 copy-start.2
  20.7 0.0 all-reduce.2.cloned.1.call-update
  20.8 0.7 copy-done.4
  21.4 0.7 convert_reduce_fusion.4
  33.5 0.7 convert_reduce_fusion
  36.8 0.0 copy-done.2
  36.8 381.6 %shard_map.55 = (f32[1024,8704]{1,0:T(8,128)}, f32[1024,1088]{1,0:T(8,128)}, f32[1024,1088]{1,0:T(8,128)}) custom-call(f32[64,8704]{1,0:T(8,128)S(1)} %copy-done.2, f32[1088,8704]{1,0:T(8,128)} %bitcast.3), custom_call_target="tpu_custom_call" | custom-call | flops 58183385088 | bytes 151519232 | tf_op jit(solution)/shard_map/pallas_call | solution.py:217
  418.4 6.4 %add.76 = f32[1024,1088]{1,0:T(8,128)} add(f32[1024,1088]{1,0:T(8,128)} %get-tuple-element.7, f32[1024,1088]{1,0:T(8,128)} %get-tuple-element.8) | non-fusion elementwise | flops 1114112 | bytes 13369344 | tf_op jit(solution)/shard_map/add | solution.py:239
  424.8 0.1 compare_convert_fusion
  424.8 0.1 fusion.24
  424.9 0.0 all-reduce.2.cloned.1.call-done
  424.9 0.0 copy-start.3
  424.9 14.8 %convolution_multiply_fusion.2 = f32[1088,2560]{1,0:T(8,128)} fusion(f32[1024,2560]{1,0:T(8,128)} %all-reduce.2.cloned.1.call-done, s32[]{:T(128)S(6)} %select_n.9, f32[512]{0:T(512)S(1)} %get-tuple-element.20, f32[1024,1088]{1,0:T(8,128)} %add.76), kind=kOutput, calls=%fused_computation.2 | convolution fusion | flops 8560476160 | bytes 18746368 | tf_op jit(solution)/shard_map/dot_general | solution.py:16
  439.7 0.0 copy-done.3
  439.7 13.9 %fusion.3 = f32[1088,2560]{1,0:T(8,128)S(1)} fusion(f32[1088,2560]{1,0:T(8,128)} %convolution_multiply_fusion.2, f32[1024,2560]{1,0:T(8,128)} %all-reduce.2.cloned.1.call-done, s32[]{:T(128)S(6)} %select_n.8, f32[512]{0:T(512)S(1)} %get-tuple-element.19, f32[1024,1088]{1,0:T(8,128)S(1)} %copy-done.3), kind=kOutput, calls=%fused_computation.7 | convolution fusion | flops 8563261440 | bytes 29887488 | tf_op jit(solution)/shard_map/dot_general | solution.py:16
  453.7 7.4 %fusion = f32[1088,2560]{1,0:T(8,128)S(1)} fusion(f32[1088,2560]{1,0:T(8,128)S(1)} %fusion.3, f32[1024,2560]{1,0:T(8,128)} %all-reduce.2.cloned.1.call-done, s32[]{:T(128)S(6)} %select_n.10, f32[256]{0:T(256)S(1)} %get-tuple-element.18, f32[1024,1088]{1,0:T(8,128)} %add.76), kind=kOutput, calls=%fused_computation.4 | convolution fusion | flops 4284416000 | bytes 26085376 | tf_op jit(solution)/shard_map/dot_general | solution.py:16
  461.1 0.0 copy-start.1
  461.1 12.0 %fusion.2 = f32[1088,2560]{1,0:T(8,128)} fusion(f32[1088,2560]{1,0:T(8,128)S(1)} %fusion, f32[1024,2560]{1,0:T(8,128)} %all-reduce.2.cloned.1.call-done, s32[]{:T(128)S(6)} %select_n.11, f32[256]{0:T(256)S(1)} %get-tuple-element.17, f32[1024,1088]{1,0:T(8,128)} %add.76), kind=kOutput, calls=%fused_computation.6 | convolution fusion | flops 4287201280 | bytes 26085376 | tf_op jit(solution)/shard_map/dot_general | solution.py:16
  473.1 0.0 copy-done.1
Async XLA Ops:
  6.5 1.9 copy-start
  6.5 418.4 %all-reduce.2.cloned.1.call-start = ((), (), s32[]{:S(2)}) async-start(), calls=%async_computation | async-start | bytes 20971520 | tf_op jit(solution)/shard_map/psum | solution.py:243
  20.7 0.7 copy-start.4
  20.7 16.1 %copy-start.2 = (f32[64,8704]{1,0:T(8,128)S(1)}, f32[64,8704]{1,0:T(8,128)}, u32[]{:S(2)}) copy-start(f32[64,8704]{1,0:T(8,128)} %x_ref.1) | copy-start | bytes 6684676
  424.9 14.8 %copy-start.3 = (f32[1024,1088]{1,0:T(8,128)S(1)}, f32[1024,1088]{1,0:T(8,128)}, u32[]{:S(2)}) copy-start(f32[1024,1088]{1,0:T(8,128)} %add.76) | copy-start | bytes 13369348
  461.1 12.0 %copy-start.1 = (f32[320,2560]{1,0:T(8,128)S(1)}, f32[320,2560]{1,0:T(8,128)}, u32[]{:S(2)}) copy-start(f32[320,2560]{1,0:T(8,128)} %param.8) | copy-start | bytes 9830404
Sparse Core Ops, SparseCore 0:
  20.9 317.8 all-reduce.1
